TPU v7x, 256 devices: a whole 4x4x8 slice. The times are simulated.
256 devices in a mesh: rep: 8 (over y, x_hi), blk: 32 (over z, x_lo, core).
Axes of the slice: x: 4 (x_hi: 2, x_lo: 2; x = x_hi * 2 + x_lo), y: 4, z: 8, core: 2. Of those that a mesh axis runs over, the one named last changes fastest.
Arguments:
- node_features: bfloat16 [65536, 256], P(('rep', 'blk')), may hold values from -6 to 6
- tile_values: bfloat16 [8, 32, 128, 128, 128], P('rep', 'blk'), may hold values from -0.09375 to 0.09375
- tile_row: int32 [8, 32, 128], P('rep', 'blk'), may hold values from 0 to 15, as said below
- tile_col: int32 [8, 32, 128], P('rep', 'blk'), may hold values from 0 to 63
- tile_count: int32 [8, 32], P('rep', 'blk'), may hold values from 16 to 128, as said below
- weight: bfloat16 [256, 256], replicated, may hold values from -0.375 to 0.375
- cotangent: bfloat16 [32, 8, 256, 256], P('blk', 'rep'), may hold values from -6 to 6
Outputs:
- layer_out: bfloat16 [32, 8, 256, 256], P('blk', 'rep')
- grad_weight: float32 [256, 256], replicated
- grad_features: bfloat16 [65536, 256], P(('rep', 'blk'))
Inputs may be any that keep to these rules, and one draw needn't show every extreme that they name: `tile_row`: within one device the live slots name distinct tile pairs. Slots 0 to tile_count - 1 of a device are live, the rest are ignored; some device has all 128 slots live.
All inputs are finite; a program needn't handle non-finite values.
Results may differ from a plain program's by a relative error of at most 0.03.
Values may be sent and summed in bfloat16 or wider, within the bound.
No kernel may reach another device: no remote copies, remote signals or barrier semaphores. Data moves between devices by JAX's collectives and lax.ppermute only.
A program may use at most 128 MiB of HBM per device.

v0:
```python
import jax
import jax.numpy as jnp
from jax import lax
from jax.sharding import PartitionSpec as P


def on_device(node_features, tile_values, tile_row, tile_col, tile_count, weight, cotangent):
    rows_dev, features = node_features.shape
    tile_block = tile_values[0, 0]
    slot_rows = tile_row[0, 0]
    slot_cols = tile_col[0, 0]
    live_count = tile_count[0, 0]
    slot_count = tile_block.shape[0]
    tile_size = tile_block.shape[1]
    rep_size = lax.axis_size("rep")
    slab_rows = rows_dev * rep_size
    slab_blocks = slab_rows // tile_size
    live_mask = (jnp.arange(slot_count, dtype=jnp.int32) < live_count).astype(jnp.float32)
    row_hot = (slot_rows[:, None] == jnp.arange(slab_blocks, dtype=jnp.int32)[None, :]).astype(
        jnp.float32
    ) * live_mask[:, None]
    gathered = lax.all_gather(node_features, "blk", axis=0, tiled=True)
    group_blocks = gathered.shape[0] // tile_size
    col_hot = (slot_cols[:, None] == jnp.arange(group_blocks, dtype=jnp.int32)[None, :]).astype(
        jnp.float32
    ) * live_mask[:, None]
    col_blocks = gathered.reshape(group_blocks, tile_size, features)
    picked = jnp.take(col_blocks, slot_cols, axis=0)
    products = jnp.einsum("tij,tjf->tif", tile_block, picked, preferred_element_type=jnp.float32)
    partial_value = (
        jnp.einsum("tk,tif->kif", row_hot, products)
        .reshape(slab_rows, features)
        .astype(jnp.bfloat16)
    )
    hidden_rows = (
        lax.psum_scatter(partial_value, "rep", scatter_dimension=0, tiled=True)
        .astype(jnp.float32)
        .astype(jnp.bfloat16)
    )
    preact = jnp.dot(hidden_rows, weight, preferred_element_type=jnp.float32)
    gating = jax.nn.sigmoid(preact)
    layer_out = (preact * gating).astype(jnp.bfloat16)
    slope_term = gating * (1.0 + preact * (1.0 - gating))
    grad_pre = (cotangent[0, 0].astype(jnp.float32) * slope_term).astype(jnp.bfloat16)
    weight_part = jnp.einsum("nf,ng->fg", hidden_rows, grad_pre, preferred_element_type=jnp.float32)
    grad_hidden = jnp.dot(grad_pre, weight.T, preferred_element_type=jnp.float32).astype(
        jnp.bfloat16
    )
    grad_slab = lax.all_gather(grad_hidden, "rep", axis=0, tiled=True)
    grad_weight = lax.psum(weight_part, ("rep", "blk"))
    grad_blocks = grad_slab.reshape(slab_blocks, tile_size, features)
    picked_rows = jnp.take(grad_blocks, slot_rows, axis=0)
    back_terms = jnp.einsum(
        "tij,tif->tjf", tile_block, picked_rows, preferred_element_type=jnp.float32
    )
    column_terms = (
        jnp.einsum("tk,tjf->kjf", col_hot, back_terms)
        .reshape(group_blocks * tile_size, features)
        .astype(jnp.bfloat16)
    )
    grad_features = (
        lax.psum_scatter(column_terms, "blk", scatter_dimension=0, tiled=True)
        .astype(jnp.float32)
        .astype(jnp.bfloat16)
    )
    return (layer_out.reshape(1, 1, rows_dev, features), grad_weight, grad_features)


def solution(mesh):
    placed = (
        P(("rep", "blk"), None),
        P("rep", "blk", None, None, None),
        P("rep", "blk", None),
        P("rep", "blk", None),
        P("rep", "blk"),
        P(),
        P("blk", "rep", None, None),
    )
    return jax.shard_map(
        on_device,
        mesh=mesh,
        in_specs=placed,
        out_specs=(P("blk", "rep", None, None), P(), P(("rep", "blk"), None)),
        check_vma=False,
    )
```

profile of v0, /device:TPU:24, one launch (start us, length us, event | category | flops | bytes accessed | tf_op | source)
XLA Modules:
  0.0 638.3 jit_solution(16897174415970150977)
XLA Ops:
  7.2 0.0 copy-start
  7.2 0.0 all-gather.3.cloned.1.call-start
  7.2 0.7 all-gather.3.cloned.1.call-update
  7.9 0.0 reduce-scatter.3.cloned.1.call-start
  8.6 0.7 fusion.32
  9.3 0.7 compare_and_fusion.1
  9.9 69.5 %all-gather.3.cloned.1.call-done = bf16[8192,256]{1,0:T(8,128)(2,1)} async-done(((bf16[256,256]{1,0:T(8,128)(2,1)}), bf16[8192,256]{1,0:T(8,128)(2,1)}) %all-gather.3.cloned.1.call-update) | async-done | bytes 4194320 | tf_op jit(solution)/shard_map/all_gather | solution.py:22
  79.4 8.8 %gather_fusion = bf16[128,128,256]{2,1,0:T(8,128)(2,1)} fusion(bf16[64,128,256]{2,1,0:T(8,128)(2,1)} %bitcast.51, s32[1024]{0:T(1024)S(1)} %pad_clamp_fusion.1), kind=kCustom, calls=%fused_computation | custom fusion | bytes 16777728 | tf_op jit(solution)/shard_map/jit(_take)/gather | solution.py:28
  88.2 11.9 %fusion.6 = bf16[128,256,128]{2,1,0:T(8,128)(2,1)} fusion(bf16[128,128,256]{2,1,0:T(8,128)(2,1)} %gather_fusion, pred[128]{0:T(512)(128)(4,1)S(1)} %compare_and_fusion.1, bf16[1,1,128,128,128]{4,3,2,1,0:T(8,128)(2,1)} %param.8), kind=kOutput, calls=%fused_computation.8 | convolution fusion | flops 1077936128 | bytes 20971648 | tf_op jit(solution)/shard_map/tij,tjf->tif/dot_general | solution.py:29
  100.1 0.0 copy-start.2
  100.1 12.4 %copy.12 = bf16[128,256,128]{1,0,2:T(8,128)(2,1)} copy(bf16[128,256,128]{2,1,0:T(8,128)(2,1)} %fusion.6) | data formatting | bytes 16777216 | tf_op jit(solution)/shard_map/tij,tjf->tif/dot_general | solution.py:29
  112.5 0.0 copy-start.4
  112.5 0.0 copy-done.2
  112.5 4.6 fusion.17
  117.1 1.4 copy.10
  118.4 0.0 reduce-scatter.3.cloned.1.call-update
  118.5 0.0 all-gather.5.cloned.1.call-start
  118.5 76.1 %reduce-scatter.3.cloned.1.call-done = bf16[256,256]{1,0:T(8,128)(2,1)} async-done(((bf16[2048,256]{1,0:T(8,128)(2,1)}), bf16[256,256]{1,0:T(8,128)(2,1)}) %reduce-scatter.3.cloned.1.call-update) | async-done | bytes 131088 | tf_op jit(solution)/shard_map/reduce_scatter | solution.py:36
  194.6 0.0 copy-done
  194.6 0.0 copy-done.4
  194.6 1.8 fusion.20
  196.5 0.9 convolution_convert_fusion
  197.4 0.0 all-gather.5.cloned.1.call-update
  197.4 0.0 all-reduce.2.cloned.1.call-start
  197.5 1.8 fusion.38
  199.3 0.0 all-reduce.2.cloned.1.call-update
  199.3 0.2 reduce-scatter.5.cloned.1.call-start
  199.6 49.1 %all-gather.5.cloned.1.call-done = bf16[2048,256]{1,0:T(8,128)(2,1)} async-done(((bf16[256,256]{1,0:T(8,128)(2,1)}), bf16[2048,256]{1,0:T(8,128)(2,1)}) %all-gather.5.cloned.1.call-update) | async-done | bytes 1048592 | tf_op jit(solution)/shard_map/all_gather | solution.py:49
  248.7 7.8 %gather_fusion.1 = bf16[128,128,256]{2,1,0:T(8,128)(2,1)} fusion(bf16[16,128,256]{2,1,0:T(8,128)(2,1)} %bitcast.50, s32[1024]{0:T(1024)S(1)} %pad_clamp_fusion), kind=kCustom, calls=%fused_computation.1 | custom fusion | bytes 16777728 | tf_op jit(solution)/shard_map/jit(_take)/gather | solution.py:52
  256.5 8.9 %fusion.4 = bf16[128,256,128]{2,1,0:T(8,128)(2,1)} fusion(bf16[128,128,256]{2,1,0:T(8,128)(2,1)} %gather_fusion.1, pred[128]{0:T(512)(128)(4,1)S(1)} %compare_and_fusion, bf16[1,1,128,128,128]{4,3,2,1,0:T(8,128)(2,1)} %param.8), kind=kOutput, calls=%fused_computation.6 | convolution fusion | flops 1077936128 | bytes 20971648 | tf_op jit(solution)/shard_map/tij,tif->tjf/dot_general | solution.py:53
  265.4 0.0 copy-start.3
  265.4 12.5 %copy.13 = bf16[128,256,128]{1,0,2:T(8,128)(2,1)} copy(bf16[128,256,128]{2,1,0:T(8,128)(2,1)} %fusion.4) | data formatting | bytes 16777216 | tf_op jit(solution)/shard_map/tij,tif->tjf/dot_general | solution.py:53
  277.8 0.0 copy-done.3
  277.8 0.0 copy-start.1
  277.8 4.7 fusion.14
  282.6 4.4 copy.11
  287.0 0.0 reduce-scatter.5.cloned.1.call-update
  287.0 217.9 %all-reduce.2.cloned.1.call-done = f32[256,256]{1,0:T(8,128)} async-done(((f32[256,256]{1,0:T(8,128)}), f32[256,256]{1,0:T(8,128)}) %all-reduce.2.cloned.1.call-update) | async-done | bytes 262160 | tf_op jit(solution)/shard_map/psum | solution.py:50
  504.9 125.2 %reduce-scatter.5.cloned.1.call-done = bf16[256,256]{1,0:T(8,128)(2,1)} async-done(((bf16[8192,256]{1,0:T(8,128)(2,1)}), bf16[256,256]{1,0:T(8,128)(2,1)}) %reduce-scatter.5.cloned.1.call-update) | async-done | bytes 131088 | tf_op jit(solution)/shard_map/reduce_scatter | solution.py:62
  630.1 1.7 copy.16
  631.7 0.0 copy-done.1
  (5 shorter events, 0.0 us)
Async XLA Ops:
  7.2 187.5 %copy-start = (bf16[256,256]{1,0:T(8,128)(2,1)S(1)}, bf16[256,256]{1,0:T(8,128)(2,1)}, u32[]{:S(2)}) copy-start(bf16[256,256]{1,0:T(8,128)(2,1)} %param.12) | copy-start | bytes 393220
  7.2 72.2 %all-gather.3.cloned.1.call-start = ((), (), s32[]{:S(2)}) async-start(), calls=%async_computation.2 | async-start | bytes 4325376 | tf_op jit(solution)/shard_map/all_gather | solution.py:22
  7.9 186.7 %reduce-scatter.3.cloned.1.call-start = ((), (), s32[]{:S(2)}) async-start(), calls=%async_computation.3 | async-start | bytes 1179648 | tf_op jit(solution)/shard_map/reduce_scatter | solution.py:36
  100.1 12.4 %copy-start.2 = (s32[1,1,128]{2,1,0:T(1,128)S(1)}, s32[1,1,128]{2,1,0:T(1,128)}, u32[]{:S(2)}) copy-start(s32[1,1,128]{2,1,0:T(1,128)} %param.9) | copy-start | bytes 1540
  112.5 82.2 %copy-start.4 = (bf16[1,1,256,256]{3,2,1,0:T(8,128)(2,1)S(1)}, bf16[1,1,256,256]{3,2,1,0:T(8,128)(2,1)}, u32[]{:S(2)}) copy-start(bf16[1,1,256,256]{3,2,1,0:T(8,128)(2,1)} %param.13) | copy-start | bytes 393220
  118.5 130.2 %all-gather.5.cloned.1.call-start = ((), (), s32[]{:S(2)}) async-start(), calls=%async_computation.5 | async-start | bytes 1179648 | tf_op jit(solution)/shard_map/all_gather | solution.py:49
  197.4 307.5 %all-reduce.2.cloned.1.call-start = ((), (), s32[]{:S(2)}) async-start(), calls=%async_computation.4 | async-start | bytes 524288 | tf_op jit(solution)/shard_map/psum | solution.py:50
  199.3 430.7 %reduce-scatter.5.cloned.1.call-start = ((), (), s32[]{:S(2)}) async-start(), calls=%async_computation.6 | async-start | bytes 4325376 | tf_op jit(solution)/shard_map/reduce_scatter | solution.py:62
  265.4 12.5 %copy-start.3 = (s32[1,1,128]{2,1,0:T(1,128)S(1)}, s32[1,1,128]{2,1,0:T(1,128)}, u32[]{:S(2)}) copy-start(s32[1,1,128]{2,1,0:T(1,128)} %param.10) | copy-start | bytes 1540
  277.8 353.9 %copy-start.1 = (bf16[256,256]{1,0:T(8,128)(2,1)S(1)}, bf16[256,256]{1,0:T(8,128)(2,1)}, u32[]{:S(2)}) copy-start(bf16[256,256]{1,0:T(8,128)(2,1)} %param.12) | copy-start | bytes 393220
Sparse Core Ops, SparseCore 0:
  9.9 69.5 all-gather.2
  118.6 76.0 reduce-scatter.2
  198.2 50.4 all-gather.4
  255.5 249.3 all-reduce.1
  508.0 122.0 reduce-scatter.4
where the time goes:
time: 639 us; the launch traced here: 638 us
  waiting for transfers between devices  539 us (84%)
  local copies, waits for them, and re-layouts  48.8 us (8%)
  matrix products  34.7 us (5%)
  between operations  14.5 us (2%)
    psum x1, waiting for transfers between devices, on_device(): grad_weight = lax.psum(weight_part, ('rep', 'blk'))  218 us
    reduce_scatter x1, waiting for transfers between devices, on_device(): lax.psum_scatter(column_terms, 'blk', scatter_dimension=0, tiled=True)  125 us
    reduce_scatter x1, waiting for transfers between devices, on_device(): lax.psum_scatter(partial_value, 'rep', scatter_dimension=0, tiled=True)  76.1 us
    all_gather x1, waiting for transfers between devices, on_device(): gathered = lax.all_gather(node_features, 'blk', axis=0, tiled=True)  69.5 us
    all_gather x1, waiting for transfers between devices, on_device(): grad_slab = lax.all_gather(grad_hidden, 'rep', axis=0, tiled=True)  49.1 us
  transfers between devices with their start and end apart: 5, of which 5 were waited for; matrix products, arithmetic and copies ran while one was open for 6% of the time, Pallas kernels for 0%

commit v1 on v0

--- a/solution.py
+++ b/solution.py
@@ -47,7 +47,7 @@
         jnp.bfloat16
     )
     grad_slab = lax.all_gather(grad_hidden, "rep", axis=0, tiled=True)
-    grad_weight = lax.psum(weight_part, ("rep", "blk"))
+    grad_weight = jnp.sum(lax.all_gather(weight_part, ("rep", "blk")), axis=0)
     grad_blocks = grad_slab.reshape(slab_blocks, tile_size, features)
     picked_rows = jnp.take(grad_blocks, slot_rows, axis=0)
     back_terms = jnp.einsum(

time: 639 us -> 873 us (1.37)
  waiting for transfers between devices: 539 us -> 752 us
  other arithmetic: 1.35 us -> 23.2 us
    all_gather x0 -> x1, waiting for transfers between devices: none -> 452 us  [on_device(): grad_weight = jnp.sum(lax.all_gather(weight_part, ('rep', 'blk')), axis=0)]
    psum x1 -> x0, waiting for transfers between devices: 218 us -> none  [on_device(): grad_weight = lax.psum(weight_part, ('rep', 'blk'))]
    reduce_sum x0 -> x1, other arithmetic: none -> 21.8 us  [on_device(): grad_weight = jnp.sum(lax.all_gather(weight_part, ('rep', 'blk')), axis=0)]
    reduce_scatter x1, waiting for transfers between devices: 125 us -> 104 us  [on_device(): lax.psum_scatter(column_terms, 'blk', scatter_dimension=0, tiled=True)]
  transfers between devices with their start and end apart: 5 -> 5, of which waited for: 5 -> 5; matrix products, arithmetic and copies ran while one was open for 6% -> 7% of each run, Pallas kernels for 0% -> 0%
where the time goes in v1:
time: 873 us; the launch traced here: 872 us
  waiting for transfers between devices  752 us (86%)
  local copies, waits for them, and re-layouts  47.1 us (5%)
  matrix products  34.7 us (4%)
  other arithmetic  23.2 us (3%)
  between operations  14.5 us (2%)
    all_gather x1, waiting for transfers between devices, on_device(): grad_weight = jnp.sum(lax.all_gather(weight_part, ('rep', 'blk')), axis=0)  452 us
    reduce_scatter x1, waiting for transfers between devices, on_device(): lax.psum_scatter(column_terms, 'blk', scatter_dimension=0, tiled=True)  104 us
    reduce_scatter x1, waiting for transfers between devices, on_device(): lax.psum_scatter(partial_value, 'rep', scatter_dimension=0, tiled=True)  76.1 us
    all_gather x1, waiting for transfers between devices, on_device(): gathered = lax.all_gather(node_features, 'blk', axis=0, tiled=True)  69.5 us
    all_gather x1, waiting for transfers between devices, on_device(): grad_slab = lax.all_gather(grad_hidden, 'rep', axis=0, tiled=True)  49.1 us
    reduce_sum x1, other arithmetic, on_device(): grad_weight = jnp.sum(lax.all_gather(weight_part, ('rep', 'blk')), axis=0)  21.8 us
  transfers between devices with their start and end apart: 5, of which 5 were waited for; matrix products, arithmetic and copies ran while one was open for 7% of the time, Pallas kernels for 0%

profile of v1, /device:TPU:24, one launch (start us, length us, event | category | flops | bytes accessed | tf_op | source)
XLA Modules:
  0.0 871.6 jit_solution(1359530656707328978)
XLA Ops:
  7.2 0.0 copy-start
  7.2 0.0 all-gather.5.cloned.1.call-start
  7.2 0.7 all-gather.5.cloned.1.call-update
  7.9 0.0 reduce-scatter.3.cloned.1.call-start
  8.6 0.7 fusion.32
  9.3 0.7 compare_and_fusion.1
  9.9 69.5 %all-gather.5.cloned.1.call-done = bf16[8192,256]{1,0:T(8,128)(2,1)} async-done(((bf16[256,256]{1,0:T(8,128)(2,1)}), bf16[8192,256]{1,0:T(8,128)(2,1)}) %all-gather.5.cloned.1.call-update) | async-done | bytes 4194320 | tf_op jit(solution)/shard_map/all_gather | solution.py:22
  79.4 8.8 %gather_fusion = bf16[128,128,256]{2,1,0:T(8,128)(2,1)} fusion(bf16[64,128,256]{2,1,0:T(8,128)(2,1)} %bitcast.52, s32[1024]{0:T(1024)S(1)} %pad_clamp_fusion.1), kind=kCustom, calls=%fused_computation | custom fusion | bytes 16777728 | tf_op jit(solution)/shard_map/jit(_take)/gather | solution.py:28
  88.2 11.9 %fusion.6 = bf16[128,256,128]{2,1,0:T(8,128)(2,1)} fusion(bf16[128,128,256]{2,1,0:T(8,128)(2,1)} %gather_fusion, pred[128]{0:T(512)(128)(4,1)S(1)} %compare_and_fusion.1, bf16[1,1,128,128,128]{4,3,2,1,0:T(8,128)(2,1)} %param.8), kind=kOutput, calls=%fused_computation.8 | convolution fusion | flops 1077936128 | bytes 20971648 | tf_op jit(solution)/shard_map/tij,tjf->tif/dot_general | solution.py:29
  100.1 0.0 copy-start.2
  100.1 12.4 %copy.12 = bf16[128,256,128]{1,0,2:T(8,128)(2,1)} copy(bf16[128,256,128]{2,1,0:T(8,128)(2,1)} %fusion.6) | data formatting | bytes 16777216 | tf_op jit(solution)/shard_map/tij,tjf->tif/dot_general | solution.py:29
  112.5 0.0 copy-start.4
  112.5 0.0 copy-done.2
  112.5 4.6 fusion.17
  117.1 1.4 copy.10
  118.4 0.0 reduce-scatter.3.cloned.1.call-update
  118.5 0.0 all-gather.7.cloned.1.call-start
  118.5 76.1 %reduce-scatter.3.cloned.1.call-done = bf16[256,256]{1,0:T(8,128)(2,1)} async-done(((bf16[2048,256]{1,0:T(8,128)(2,1)}), bf16[256,256]{1,0:T(8,128)(2,1)}) %reduce-scatter.3.cloned.1.call-update) | async-done | bytes 131088 | tf_op jit(solution)/shard_map/reduce_scatter | solution.py:36
  194.6 0.0 copy-done
  194.6 0.0 copy-done.4
  194.6 1.8 fusion.20
  196.5 0.9 convolution_convert_fusion
  197.4 0.0 all-gather.7.cloned.1.call-update
  197.4 0.0 all-gather.9.cloned.1.call-start
  197.4 1.8 fusion.38
  199.3 0.0 all-gather.9.cloned.1.call-update
  199.3 0.2 reduce-scatter.5.cloned.1.call-start
  199.6 49.1 %all-gather.7.cloned.1.call-done = bf16[2048,256]{1,0:T(8,128)(2,1)} async-done(((bf16[256,256]{1,0:T(8,128)(2,1)}), bf16[2048,256]{1,0:T(8,128)(2,1)}) %all-gather.7.cloned.1.call-update) | async-done | bytes 1048592 | tf_op jit(solution)/shard_map/all_gather | solution.py:49
  248.7 7.8 gather_fusion.1
  256.5 8.9 %fusion.4 = bf16[128,256,128]{2,1,0:T(8,128)(2,1)} fusion(bf16[128,128,256]{2,1,0:T(8,128)(2,1)} %gather_fusion.1, pred[128]{0:T(512)(128)(4,1)S(1)} %compare_and_fusion, bf16[1,1,128,128,128]{4,3,2,1,0:T(8,128)(2,1)} %param.8), kind=kOutput, calls=%fused_computation.6 | convolution fusion | flops 1077936128 | bytes 20971648 | tf_op jit(solution)/shard_map/tij,tif->tjf/dot_general | solution.py:53
  265.4 0.0 copy-start.3
  265.4 12.4 %copy.13 = bf16[128,256,128]{1,0,2:T(8,128)(2,1)} copy(bf16[128,256,128]{2,1,0:T(8,128)(2,1)} %fusion.4) | data formatting | bytes 16777216 | tf_op jit(solution)/shard_map/tij,tif->tjf/dot_general | solution.py:53
  277.8 0.0 copy-done.3
  277.8 4.8 fusion.14
  282.6 4.4 copy.11
  287.0 0.0 reduce-scatter.5.cloned.1.call-update
  287.0 451.8 %all-gather.9.cloned.1.call-done = f32[65536,256]{1,0:T(8,128)} async-done(((f32[256,256]{1,0:T(8,128)}), f32[65536,256]{1,0:T(8,128)}) %all-gather.9.cloned.1.call-update) | async-done | bytes 67108880 | tf_op jit(solution)/shard_map/all_gather | solution.py:50
  738.8 0.0 copy-start.1
  738.8 21.8 %reduce_sum.9 = f32[256,256]{1,0:T(8,128)} reduce(f32[256,256,256]{2,1,0:T(8,128)} %bitcast.12, f32[]{:T(128)} %constant.28.clone.1), dimensions={0}, to_apply=%region_1.2 | reduce | flops 16711680 | bytes 67371008 | tf_op jit(solution)/shard_map/reduce_sum | solution.py:50
  760.6 104.4 %reduce-scatter.5.cloned.1.call-done = bf16[256,256]{1,0:T(8,128)(2,1)} async-done(((bf16[8192,256]{1,0:T(8,128)(2,1)}), bf16[256,256]{1,0:T(8,128)(2,1)}) %reduce-scatter.5.cloned.1.call-update) | async-done | bytes 131088 | tf_op jit(solution)/shard_map/reduce_scatter | solution.py:62
  865.0 0.0 copy-done.1
  (5 shorter events, 0.0 us)
Async XLA Ops:
  7.2 187.5 %copy-start = (bf16[256,256]{1,0:T(8,128)(2,1)S(1)}, bf16[256,256]{1,0:T(8,128)(2,1)}, u32[]{:S(2)}) copy-start(bf16[256,256]{1,0:T(8,128)(2,1)} %param.12) | copy-start | bytes 393220
  7.2 72.2 %all-gather.5.cloned.1.call-start = ((), (), s32[]{:S(2)}) async-start(), calls=%async_computation.2 | async-start | bytes 4325376 | tf_op jit(solution)/shard_map/all_gather | solution.py:22
  7.9 186.7 %reduce-scatter.3.cloned.1.call-start = ((), (), s32[]{:S(2)}) async-start(), calls=%async_computation.3 | async-start | bytes 1179648 | tf_op jit(solution)/shard_map/reduce_scatter | solution.py:36
  100.1 12.4 %copy-start.2 = (s32[1,1,128]{2,1,0:T(1,128)S(1)}, s32[1,1,128]{2,1,0:T(1,128)}, u32[]{:S(2)}) copy-start(s32[1,1,128]{2,1,0:T(1,128)} %param.9) | copy-start | bytes 1540
  112.5 82.2 %copy-start.4 = (bf16[1,1,256,256]{3,2,1,0:T(8,128)(2,1)S(1)}, bf16[1,1,256,256]{3,2,1,0:T(8,128)(2,1)}, u32[]{:S(2)}) copy-start(bf16[1,1,256,256]{3,2,1,0:T(8,128)(2,1)} %param.13) | copy-start | bytes 393220
  118.5 130.2 %all-gather.7.cloned.1.call-start = ((), (), s32[]{:S(2)}) async-start(), calls=%async_computation.4 | async-start | bytes 1179648 | tf_op jit(solution)/shard_map/all_gather | solution.py:49
  197.4 541.4 %all-gather.9.cloned.1.call-start = ((), (), s32[]{:S(2)}) async-start(), calls=%async_computation.6 | async-start | bytes 67371008 | tf_op jit(solution)/shard_map/all_gather | solution.py:50
  199.3 665.7 %reduce-scatter.5.cloned.1.call-start = ((), (), s32[]{:S(2)}) async-start(), calls=%async_computation.5 | async-start | bytes 4325376 | tf_op jit(solution)/shard_map/reduce_scatter | solution.py:62
  265.4 12.4 %copy-start.3 = (s32[1,1,128]{2,1,0:T(1,128)S(1)}, s32[1,1,128]{2,1,0:T(1,128)}, u32[]{:S(2)}) copy-start(s32[1,1,128]{2,1,0:T(1,128)} %param.10) | copy-start | bytes 1540
  738.8 126.3 %copy-start.1 = (bf16[256,256]{1,0:T(8,128)(2,1)S(1)}, bf16[256,256]{1,0:T(8,128)(2,1)}, u32[]{:S(2)}) copy-start(bf16[256,256]{1,0:T(8,128)(2,1)} %param.12) | copy-start | bytes 393220
Sparse Core Ops, SparseCore 0:
  9.9 69.5 all-gather.4
  118.6 76.0 reduce-scatter.2
  198.2 50.4 all-gather.6
  251.2 487.5 all-gather.8
  741.9 123.1 reduce-scatter.4
